TPU v7x, 32 devices: a whole 2x2x4 slice. The times are simulated.
32 devices in a mesh: shot: 2 (over core), probe: 16 (over z, y, x).
Axes of the slice: x: 2, y: 2, z: 4, core: 2. Of those that a mesh axis runs over, the one named last changes fastest.
Arguments:
- probes: float32 [32, 256, 512], P('probe'), may hold values from -6 to 6
- coarse_sample: float32 [32, 256, 512], P('probe', 'shot'), may hold values from -6 to 6
- coefficient: float32 [256, 512], replicated, may hold values from 0.05 to 0.45
- receiver: float32 [256, 512], replicated, may hold values from 0.05 to 0.5
- checkpoints: float32 [4, 2, 256, 512], P('shot', None, 'probe'), may hold values from -6 to 6
- encodings: int32 [4, 256], P('shot'), may hold values from -1 to 1, as said below
- wavelet: float32 [3, 256], replicated, may hold values from -6 to 6
- bounds: int32 [33], replicated, may hold values from 0 to 256, as said below
Outputs:
- samples: float32 [32, 256, 512], P('probe', 'shot')
Inputs may be any that keep to these rules, and one draw needn't show every extreme that they name: `encodings`: every entry is -1 or 1. bounds[0] = 0 and bounds[32] = 256; the entries rise strictly; blocks 2 i and 2 i + 1 together hold exactly 16 rows.
All inputs are finite; a program needn't handle non-finite values.
Results may differ from a plain program's by a relative error of at most 0.000094.
Values sent between devices are 32-bit elements; how exact they have to be, the bound alone decides.
A program may use at most 128 MiB of HBM per device.

v0:
```python
import functools

import jax
import jax.numpy as jnp
from jax import lax
from jax.experimental import pallas as pl
from jax.experimental.pallas import tpu as pltpu
from jax.sharding import PartitionSpec as P

MESH = pl.DeviceIdType.MESH
SUB = 8
LANE = 128
INNER = 4


def kernel(
    num_shot_devices,
    num_probe_devices,
    bounds_ref,
    encodings_ref,
    wavelet_ref,
    probes_hbm,
    coarse_hbm,
    coefficient_hbm,
    receiver_hbm,
    checkpoints_hbm,
    out_ref,
    gathered,
    probes_in,
    coarse_in,
    coefficient_in,
    receiver_in,
    coef,
    centre,
    weight,
    vec,
    um,
    u0,
    u1,
    u2,
    u3,
    d1,
    d2,
    d3,
    e4,
    e3,
    e2,
    total,
    flat,
    partial,
    inverse,
    parity_out,
    source,
    load_sem,
    own_sem,
    recv_sem,
    send_sem,
    line_sem,
    swap_send,
    swap_recv,
):
    members, _, chunk, width = checkpoints_hbm.shape
    num_probes, num_rows, _ = probes_hbm.shape
    out_rows = coarse_hbm.shape[1]
    tiles = num_rows // SUB
    cols = [pl.ds(c * LANE, LANE) for c in range(width // LANE)]
    steps = wavelet_ref.shape[0]
    line = num_probe_devices // INNER
    flags = num_probe_devices * 2

    shot = lax.axis_index("shot")
    mine = lax.axis_index("probe")
    z = mine // INNER
    a = mine % INNER
    high, low = a // 2, a % 2
    right = 2 * low + (1 - high)
    left = 2 * (1 - low) + high

    places = {"a": a, "right": right, "left": left, "far": 3 - a}
    ids = {
        (dz, name): (z + dz) * INNER + place
        for dz in range(1 - line, line)
        for name, place in places.items()
    }
    exists = {dz: (z + dz >= 0) & (z + dz < line) for dz in range(1 - line, line)}
    def slot(m, src, t):
        first = pl.multiple_of((src * 2 + t) * chunk, chunk)
        return gathered.at[m, :, pl.ds(first, chunk), :]

    def own_copy(m, t):
        first = pl.multiple_of((mine * 2 + t) * chunk, chunk)
        return [
            pltpu.make_async_copy(
                checkpoints_hbm.at[m, t, :, c],
                gathered.at[m, i, pl.ds(first, chunk), :],
                own_sem.at[(m * 2 + t) * len(cols) + i],
            )
            for i, c in enumerate(cols)
        ]

    for m in range(members):
        for t in range(2):
            for copy in own_copy(m, t):
                copy.start()

    count = len(cols)
    load_probes = [
        pltpu.make_async_copy(probes_hbm.at[:, :, c], probes_in.at[:, i], load_sem.at[i])
        for i, c in enumerate(cols)
    ]
    load_coefficient = [
        pltpu.make_async_copy(coefficient_hbm.at[:, c], coefficient_in.at[i], load_sem.at[count + i])
        for i, c in enumerate(cols)
    ]
    load_receiver = [
        pltpu.make_async_copy(receiver_hbm.at[:, c], receiver_in.at[i], load_sem.at[2 * count + i])
        for i, c in enumerate(cols)
    ]
    load_coarse = [pltpu.make_async_copy(coarse_hbm, coarse_in, load_sem.at[3 * count])]
    for load in load_coefficient + load_receiver + load_probes + load_coarse:
        load.start()

    barrier = pltpu.get_barrier_semaphore()

    def greet(device):
        pl.semaphore_signal(barrier, inc=1, device_id=device, device_id_type=MESH)

    greet({"probe": ids[0, "right"]})
    greet({"probe": ids[0, "left"]})

    for dz in range(1 - line, line):
        if dz:

            @pl.when(exists[dz])
            def _(dz=dz):
                greet({"probe": ids[dz, "a"]})

    for away in range(1, num_shot_devices):
        greet({"shot": (shot + away) % num_shot_devices})
    pl.semaphore_wait(barrier, line - 1 + 2 + num_shot_devices - 1)

    sent = []

    def send(m, src, t, target, sem, cond=None):
        def copy():
            return pltpu.make_async_remote_copy(
                src_ref=slot(m, ids[src], t),
                dst_ref=slot(m, ids[src], t),
                send_sem=sem(),
                recv_sem=recv_sem.at[m * flags + ids[src] * 2 + t],
                device_id={"probe": ids[target]},
                device_id_type=MESH,
            )

        copy().start()
        sent.append((copy, cond))

    def arrive(m, src, t):
        pltpu.make_async_remote_copy(
            src_ref=slot(m, ids[src], t),
            dst_ref=slot(m, ids[src], t),
            send_sem=send_sem.at[m * flags + ids[src] * 2 + t],
            recv_sem=recv_sem.at[m * flags + ids[src] * 2 + t],
            device_id={"probe": ids[0, "right"]},
            device_id_type=MESH,
        ).wait_recv()

    def ring(m, src, t, name, cond=None):
        lane = 0 if name == "right" else 1
        send(
            m,
            src,
            t,
            (0, name),
            lambda: send_sem.at[(lane * members + m) * flags + ids[src] * 2 + t],
            cond,
        )

    def spread(m, src, cond=None):
        for t in (0, 1):
            ring(m, src, t, "right", cond)
            ring(m, src, 1 - t, "left", cond)

    def begin(m):
        for t in range(2):
            for copy in own_copy(m, t):
                copy.wait()
        for k in range(1, line):
            for dz in (k, -k):

                @pl.when(exists[dz])
                def _(dz=dz):
                    for t in (0, 1):
                        index = ((dz + line - 1) * members + m) * 2 + t
                        send(m, (0, "a"), t, (dz, "a"), lambda index=index: line_sem.at[index], exists[dz])

        spread(m, (0, "a"))

    def column(m, k):
        for dz, here in sides(k):

            @pl.when(here)
            def _(dz=dz, here=here):
                for t in (0, 1):
                    arrive(m, (dz, "a"), t)
                spread(m, (dz, "a"), here)

    def sides(k):
        if k == 0:
            return ((0, None),)
        return ((-k, exists[-k]), (k, exists[k]))

    def guarded(cond, fun):
        if cond is None:
            fun()
        else:
            pl.when(cond)(fun)

    def relay(m, k):
        for dz, cond in sides(k):

            def run(dz=dz, cond=cond):
                arrive(m, (dz, "left"), 0)
                ring(m, (dz, "left"), 0, "right", cond)
                arrive(m, (dz, "right"), 1)
                ring(m, (dz, "right"), 1, "left", cond)

            guarded(cond, run)

    def finish(m, k):
        for dz, cond in sides(k):

            def run(dz=dz):
                arrive(m, (dz, "left"), 1)
                arrive(m, (dz, "right"), 0)
                arrive(m, (dz, "far"), 0)
                arrive(m, (dz, "far"), 1)

            guarded(cond, run)

    def gather_steps(m):
        plan = []
        for k in range(1, line):
            plan.append(lambda k=k: column(m, k))
        for k in range(line):
            plan.append(lambda k=k: relay(m, k))
        return plan

    def gather_end(m):
        for k in range(line):
            finish(m, k)

    for m in range(members):
        begin(m)

    row_in_tile = lax.broadcasted_iota(jnp.int32, (SUB, LANE), 0)
    lane_index = lax.broadcasted_iota(jnp.int32, (SUB, LANE), 1)
    at_first = lane_index == 0
    at_last = lane_index == LANE - 1

    def parity_of(rows):
        count = jnp.zeros((SUB, LANE), jnp.int32)
        for b in range(1, bounds_ref.shape[0] - 1):
            count = count + jnp.where(rows >= bounds_ref[b], 1, 0)
        return count % 2

    def prepare_sources():
        shots = wavelet_ref.shape[1]
        spacing = width // shots
        k = lax.broadcasted_iota(jnp.int32, (shots, width), 0)
        position = k * width // shots + spacing // 2
        column_index = lax.broadcasted_iota(jnp.int32, (shots, width), 1)
        onehot = jnp.where(position == column_index, 1.0, 0.0)
        for m in range(members):
            amplitude = encodings_ref[m : m + 1, :].astype(jnp.float32) * wavelet_ref[...]
            source[m, 0:steps, :] = jnp.dot(
                amplitude,
                onehot,
                precision=lax.Precision.HIGHEST,
                preferred_element_type=jnp.float32,
            )

    def strided(j):
        return pl.ds(j, SUB, stride=tiles)

    def prepare_fields(first, last):
        def body(j, carry):
            parity = parity_of(row_in_tile * tiles + j)
            for i, c in enumerate(cols):
                value = coefficient_in[i, strided(j), :]
                seen = receiver_in[i, strided(j), :]
                coef[j, :, c] = value
                centre[j, :, c] = 2.0 - 4.0 * value
                weight[j, :, c] = value * (seen * seen)
                for p in range(num_probes):
                    vec[p, j, :, c] = jnp.where(
                        parity == p % 2, probes_in[p, i, strided(j), :], 0.0
                    )
            return carry

        lax.fori_loop(first, last, body, 0, unroll=2)

    def prepare_out():
        def body(i, carry):
            first = shot * out_rows + i * SUB
            parity_out[i] = parity_of(row_in_tile + first)
            for n, c in enumerate(cols):
                rows = pl.ds(pl.multiple_of(first, SUB), SUB)
                inverse[i, :, c] = 1.0 / coefficient_in[n, rows, :]
            return carry

        lax.fori_loop(0, out_rows // SUB, body, 0, unroll=2)

    def halo(field):
        for c in cols:
            above = pltpu.roll(field[tiles, :, c], 1, 0)
            field[0, :, c] = jnp.where(row_in_tile == 0, 0.0, above)
            below = pltpu.roll(field[1, :, c], SUB - 1, 0)
            field[tiles + 1, :, c] = jnp.where(row_in_tile == SUB - 1, 0.0, below)

    def around(field, j):
        here = [field[j + 1, :, c] for c in cols]
        fore = [pltpu.roll(x, 1, 1) for x in here]
        back = [pltpu.roll(x, LANE - 1, 1) for x in here]
        near = []
        for i, c in enumerate(cols):
            west = jnp.where(at_first, fore[i - 1] if i else 0.0, fore[i])
            east = jnp.where(at_last, back[i + 1] if i + 1 < len(cols) else 0.0, back[i])
            near.append((field[j, :, c] + field[j + 2, :, c]) + (west + east))
        return here, near

    def advance(field, before, j):
        here, near = around(field, j)
        moved = []
        for i, c in enumerate(cols):
            value = centre[j, :, c] * here[i] + coef[j, :, c] * near[i]
            if before is not None:
                value = value - before(j, c)
            moved.append(value)
        return moved

    def inner(field):
        return lambda j, c: field[j + 1, :, c]

    def convert(m):
        per = tiles // chunk
        for block in range(per):

            def body(r, carry, block=block):
                j = block * chunk + r
                for i, c in enumerate(cols):
                    um[j, :, c] = gathered[
                        m, i, pl.ds((block * 2) * chunk + r, SUB, stride=2 * tiles), :
                    ]
                    value = gathered[
                        m, i, pl.ds((block * 2 + 1) * chunk + r, SUB, stride=2 * tiles), :
                    ]
                    u0[j + 1, :, c] = value
                    for p in range(num_probes):
                        d1[p, j + 1, :, c] = vec[p, j, :, c] * value
                return carry

            lax.fori_loop(0, chunk, body, 0, unroll=2)
        halo(u0)
        for p in range(num_probes):
            halo(d1.at[p])

    def forward(m, t):
        field = (u0, u1, u2)[t]
        before = (lambda j, c: um[j, :, c], inner(u0), inner(u1))[t]
        result = (u1, u2, u3)[t]
        delta = (d1, d2, d3)[t]
        delta_before = (None, d1, d2)[t]
        delta_next = (d2, d3, e4)[t]

        def body(j, first):
            moved = advance(field, before, j)
            if first:
                for i, c in enumerate(cols):
                    row = jnp.broadcast_to(source[m, t : t + 1, c], (SUB, LANE))
                    moved[i] = moved[i] + jnp.where(row_in_tile == SUB // 2, row, 0.0)
            for i, c in enumerate(cols):
                result[j + 1, :, c] = moved[i]
            for p in range(num_probes):
                prior = None if delta_before is None else inner(delta_before.at[p])
                step = advance(delta.at[p], prior, j)
                for i, c in enumerate(cols):
                    value = step[i] + vec[p, j, :, c] * moved[i]
                    if t < 2:
                        delta_next[p, j + 1, :, c] = value
                    else:
                        value = weight[j, :, c] * value
                        delta_next[p, j + 1, :, c] = value
                        gain = moved[i] * value
                        if m:
                            gain = total[p, j, :, c] + gain
                        total[p, j, :, c] = gain

        body(0, True)

        def rest(j, carry):
            body(j, False)
            return carry

        lax.fori_loop(1, tiles, rest, 0, unroll=4)
        if t < 2:
            halo(result)
        for p in range(num_probes):
            halo(delta_next.at[p])

    def adjoint(m, t, which):
        field = (e4, e3, e2)[t]
        before = (None, e4, e3)[t]
        result = (e3, e2, None)[t]
        delta = (d3, d2, d1)[t]
        level = (u2, u1, u0)[t]

        def body(j, carry):
            for p in which:
                prior = None if before is None else inner(before.at[p])
                step = advance(field.at[p], prior, j)
                for i, c in enumerate(cols):
                    value = step[i] + weight[j, :, c] * delta[p, j + 1, :, c]
                    if result is not None:
                        result[p, j + 1, :, c] = value
                    gain = total[p, j, :, c] + level[j + 1, :, c] * value
                    if result is None and m == members - 1:
                        flat[p, i, strided(j), :] = gain
                    else:
                        total[p, j, :, c] = gain
            return carry

        lax.fori_loop(0, tiles, body, 0, unroll=4)
        if result is not None:
            for p in which:
                halo(result.at[p])

    def swap(p):
        copies = []
        for away in range(1, num_shot_devices):
            other = (shot + away) % num_shot_devices
            copies.append(
                pltpu.make_async_remote_copy(
                    src_ref=flat.at[p, :, pl.ds(pl.multiple_of(other * out_rows, SUB), out_rows), :],
                    dst_ref=partial.at[away - 1, p],
                    send_sem=swap_send.at[away - 1, p],
                    recv_sem=swap_recv.at[away - 1, p],
                    device_id={"shot": other},
                    device_id_type=MESH,
                )
            )
        return copies

    def combine(p):
        def body(i, carry):
            first = pl.multiple_of(shot * out_rows + i * SUB, SUB)
            local = pl.ds(pl.multiple_of(i * SUB, SUB), SUB)
            keep = parity_out[i] != p % 2
            for n, c in enumerate(cols):
                value = flat[p, n, pl.ds(first, SUB), :]
                for away in range(1, num_shot_devices):
                    value = value + partial[away - 1, p, n, local, :]
                value = value * inverse[i, :, c] - coarse_in[p, local, c]
                out_ref[p, local, c] = jnp.where(keep, value, 0.0)
            return carry

        lax.fori_loop(0, out_rows // SUB, body, 0)

    everything = tuple(range(num_probes))
    prepare_sources()
    for load in load_coefficient + load_receiver + load_probes:
        load.wait()
    work = []
    for q in range(4):
        work.append(lambda q=q: prepare_fields(q * tiles // 4, (q + 1) * tiles // 4))
    work.append(prepare_out)
    for step in gather_steps(0):
        step()
        if work:
            work.pop(0)()
    for rest in work:
        rest()
    load_coarse[0].wait()
    copies = [None] * num_probes
    for m in range(members):
        plan = gather_steps(m + 1) if m + 1 < members else []
        if plan:
            for _ in range(line - 1):
                plan.pop(0)()
        gather_end(m)
        stages = [lambda: convert(m)]
        stages += [lambda t=t: forward(m, t) for t in range(3)]
        stages += [lambda t=t: adjoint(m, t, everything) for t in range(2)]
        if m < members - 1:
            stages.append(lambda: adjoint(m, 2, everything))
        for stage in stages:
            stage()
            if plan:
                plan.pop(0)()
        for step in plan:
            step()
    for p in everything:
        adjoint(members - 1, 2, (p,))
        copies[p] = swap(p)
        for copy in copies[p]:
            copy.start()
    for p in everything:
        for copy in copies[p]:
            copy.wait_recv()
        combine(p)
    for p in everything:
        for copy in copies[p]:
            copy.wait_send()
    for copy, cond in sent:
        guarded(cond, lambda copy=copy: copy().wait_send())


def on_device(
    num_shot_devices,
    num_probe_devices,
    probes,
    coarse_sample,
    coefficient,
    receiver,
    checkpoints,
    encodings,
    wavelet,
    bounds,
):
    members, levels, chunk, width = checkpoints.shape
    num_probes, num_rows, _ = probes.shape
    out_rows = coarse_sample.shape[1]
    tiles = num_rows // SUB
    groups = width // LANE
    line = num_probe_devices // INNER
    f32 = jnp.float32

    def plain(*lead):
        return pltpu.VMEM((*lead, tiles, SUB, width), f32)

    def ringed(*lead):
        return pltpu.VMEM((*lead, tiles + 2, SUB, width), f32)

    others = num_shot_devices - 1
    anywhere = pl.BlockSpec(memory_space=pl.ANY)
    vmem = pl.BlockSpec(memory_space=pltpu.VMEM)
    return pl.pallas_call(
        functools.partial(kernel, num_shot_devices, num_probe_devices),
        out_shape=jax.ShapeDtypeStruct(coarse_sample.shape, f32),
        in_specs=[pl.BlockSpec(memory_space=pltpu.SMEM), vmem, vmem] + [anywhere] * 5,
        out_specs=vmem,
        scratch_shapes=[
            pltpu.VMEM((members, groups, levels * num_rows, LANE), f32),
            pltpu.VMEM((num_probes, groups, num_rows, LANE), f32),
            pltpu.VMEM(coarse_sample.shape, f32),
            pltpu.VMEM((groups, num_rows, LANE), f32),
            pltpu.VMEM((groups, num_rows, LANE), f32),
            plain(),
            plain(),
            plain(),
            plain(num_probes),
            plain(),
            ringed(),
            ringed(),
            ringed(),
            ringed(),
            ringed(num_probes),
            ringed(num_probes),
            ringed(num_probes),
            ringed(num_probes),
            ringed(num_probes),
            ringed(num_probes),
            plain(num_probes),
            pltpu.VMEM((num_probes, groups, num_rows, LANE), f32),
            pltpu.VMEM((others, num_probes, groups, out_rows, LANE), f32),
            pltpu.VMEM((out_rows // SUB, SUB, width), f32),
            pltpu.VMEM((out_rows // SUB, SUB, LANE), jnp.int32),
            pltpu.VMEM((members, SUB, width), f32),
            pltpu.SemaphoreType.DMA((3 * groups + 1,)),
            pltpu.SemaphoreType.DMA((members * levels * groups,)),
            pltpu.SemaphoreType.DMA((members * num_probe_devices * levels,)),
            pltpu.SemaphoreType.DMA((2 * members * num_probe_devices * levels,)),
            pltpu.SemaphoreType.DMA(((2 * line - 1) * members * levels,)),
            pltpu.SemaphoreType.DMA((others, num_probes)),
            pltpu.SemaphoreType.DMA((others, num_probes)),
        ],
        compiler_params=pltpu.CompilerParams(
            collective_id=0, has_side_effects=True, vmem_limit_bytes=60 * 1024 * 1024
        ),
    )(
        bounds,
        encodings,
        wavelet,
        probes,
        coarse_sample,
        coefficient,
        receiver,
        checkpoints,
    )


def solution(mesh):
    return jax.shard_map(
        functools.partial(on_device, mesh.shape["shot"], mesh.shape["probe"]),
        mesh=mesh,
        in_specs=(
            P("probe", None, None),
            P("probe", "shot", None),
            P(),
            P(),
            P("shot", None, "probe", None),
            P("shot", None),
            P(),
            P(),
        ),
        out_specs=P("probe", "shot", None),
        check_vma=False,
    )
```

profile of v0, /device:TPU:1, one launch (start us, length us, event | category | flops | bytes accessed | tf_op | source)
XLA Modules:
  0.0 50.9 jit_solution(14718634163924049558)
XLA Ops:
  0.0 49.0 %shard_map.82 = f32[2,128,512]{2,1,0:T(8,128)} custom-call(s32[33]{0:T(128)} %bounds_ref.1, s32[2,256]{1,0:T(2,128)} %encodings_ref.1, f32[3,256]{1,0:T(4,128)} %wavelet_ref.1, f32[2,256,512]{2,1,0:T(8,128)} %probes_hbm.1, f32[2,128,512]{2,1,0:T(8,128)} %coarse_hbm.1, f32[256,512]{1,0:T(8,128)} %coefficient_hbm.1, f32[256,512]{1,0:T(8,128)} %receiver_hbm.1, ...), custom_call_target="tpu_custom_call" | custom-call | tf_op jit(solution)/shard_map/pallas_call | solution.py:547
  49.0 1.9 %copy.10 = f32[2,128,512]{2,1,0:T(8,128)} copy(f32[2,128,512]{2,1,0:T(8,128)} %shard_map.82) | data formatting | bytes 1048576
where the time goes:
time: 51.1 us; the launch traced here: 50.9 us
  Pallas kernels  49 us (96%)
  local copies, waits for them, and re-layouts  1.87 us (4%)
    pallas_call x1, Pallas kernels, on_device(): pl.pallas_call(functools.partial(kernel, num_shot_devices, num_probe_devi...  49 us
    unnamed x1, local copies, waits for them, and re-layouts  1.87 us

commit v1 on v0

v1 whole, which is shorter than its diff:
```python
import functools

import jax
import jax.numpy as jnp
from jax import lax
from jax.experimental import pallas as pl
from jax.experimental.pallas import tpu as pltpu
from jax.sharding import PartitionSpec as P

MESH = pl.DeviceIdType.MESH
SUB = 8
LANE = 128
INNER = 4
UNROLL = 4


def kernel(
    num_shot_devices,
    num_probe_devices,
    bounds_ref,
    encodings_ref,
    wavelet_ref,
    probes_hbm,
    coarse_hbm,
    coefficient_hbm,
    receiver_hbm,
    checkpoints_hbm,
    out_hbm,
    own_in,
    own,
    probes_in,
    coarse_in,
    coefficient_in,
    receiver_in,
    inverse,
    spread_table,
    collect_table,
    parity_in,
    parity_out,
    coef,
    centre,
    weight,
    vec,
    um,
    u0,
    u1,
    u2,
    u3,
    d1,
    d2,
    d3,
    e4,
    e3,
    e2,
    total,
    packed,
    partial,
    result_out,
    source,
    load_sem,
    own_sem,
    recv_sem,
    send_sem,
    line_sem,
    pack_sem,
    out_sem,
    swap_send,
    swap_recv,
):
    members, levels, chunk, width = checkpoints_hbm.shape
    num_probes, num_rows, _ = probes_hbm.shape
    out_rows = coarse_hbm.shape[1]
    tiles = num_rows // SUB
    groups = width // LANE
    cols = [pl.ds(c * LANE, LANE) for c in range(groups)]
    steps = wavelet_ref.shape[0]
    line = num_probe_devices // INNER
    flags = num_probe_devices * 2
    share = SUB // num_shot_devices
    part_tiles = tiles // num_shot_devices
    block = min(8, part_tiles)
    rows_of_block = block * SUB

    shot = lax.axis_index("shot")
    mine = lax.axis_index("probe")
    z = mine // INNER
    a = mine % INNER
    high, low = a // 2, a % 2
    right = 2 * low + (1 - high)
    left = 2 * (1 - low) + high

    places = {"a": a, "right": right, "left": left, "far": 3 - a}
    ids = {
        (dz, name): (z + dz) * INNER + place
        for dz in range(1 - line, line)
        for name, place in places.items()
    }
    exists = {dz: (z + dz >= 0) & (z + dz < line) for dz in range(1 - line, line)}
    def slot(m, src, t):
        first = src * chunk
        sub = first // tiles
        tile = first % tiles
        if t:
            return u0.at[m, pl.ds(tile + 1, chunk), sub, :]
        return um.at[m, pl.ds(tile, chunk), sub, :]

    def own_copy(m, t):
        return pltpu.make_async_copy(own.at[m, t], slot(m, mine, t), own_sem.at[m * 2 + t])

    load_own = pltpu.make_async_copy(checkpoints_hbm, own_in, load_sem.at[0])
    load_own.start()

    def strided_load(src, dst, base):
        return [
            pltpu.make_async_copy(src.at[pl.ds(k * tiles, tiles), :], dst.at[:, k, :], load_sem.at[base + k])
            for k in range(SUB)
        ]

    load_probes = [
        copy
        for p in range(num_probes)
        for copy in strided_load(probes_hbm.at[p], probes_in.at[p], 1 + p * SUB)
    ]
    base = 1 + num_probes * SUB
    load_coefficient = strided_load(coefficient_hbm, coefficient_in, base)
    load_receiver = strided_load(receiver_hbm, receiver_in, base + SUB)
    base = base + 2 * SUB
    load_out = []
    for k in range(num_shot_devices):
        for e in range(share):
            first = pl.multiple_of(e * tiles + k * part_tiles, SUB)
            near = pl.multiple_of(shot * out_rows + e * tiles + k * part_tiles, SUB)
            load_out.append(
                pltpu.make_async_copy(
                    coefficient_hbm.at[pl.ds(near, part_tiles), :],
                    inverse.at[:, k * share + e, :],
                    load_sem.at[base],
                )
            )
            base += 1
            for p in range(num_probes):
                load_out.append(
                    pltpu.make_async_copy(
                        coarse_hbm.at[p, pl.ds(first, part_tiles), :],
                        coarse_in.at[p, :, k * share + e, :],
                        load_sem.at[base],
                    )
                )
                base += 1
    for load in load_probes + load_coefficient + load_receiver + load_out:
        load.start()

    barrier = pltpu.get_barrier_semaphore()

    def greet(device):
        pl.semaphore_signal(barrier, inc=1, device_id=device, device_id_type=MESH)

    greet({"probe": ids[0, "right"]})
    greet({"probe": ids[0, "left"]})

    for dz in range(1 - line, line):
        if dz:

            @pl.when(exists[dz])
            def _(dz=dz):
                greet({"probe": ids[dz, "a"]})

    for away in range(1, num_shot_devices):
        greet({"shot": (shot + away) % num_shot_devices})

    def build_tables():
        def body(b, carry):
            rows = pl.ds(pl.multiple_of(b * LANE, LANE), LANE)
            row = lax.broadcasted_iota(jnp.int32, (LANE, width), 0) + b * LANE
            col = lax.broadcasted_iota(jnp.int32, (LANE, width), 1)
            place = groups * (col % LANE) + col // LANE
            spread_table[rows, :] = jnp.where(row == place, 1.0, 0.0).astype(jnp.bfloat16)
            place = groups * (row % LANE) + row // LANE
            collect_table[rows, :] = jnp.where(col == place, 1.0, 0.0).astype(jnp.bfloat16)
            return carry

        lax.fori_loop(0, groups, body, 0)

    def shuffle(x, table):
        high = x.astype(jnp.bfloat16)
        rest = x - high.astype(jnp.float32)
        middle = rest.astype(jnp.bfloat16)
        low = (rest - middle.astype(jnp.float32)).astype(jnp.bfloat16)
        moved = [
            jnp.dot(piece, table[...], preferred_element_type=jnp.float32)
            for piece in (high, middle, low)
        ]
        return moved[0] + (moved[1] + moved[2])

    build_tables()
    load_own.wait()
    count = members * levels * chunk
    own[...] = shuffle(own_in[...].reshape(count, width), spread_table).reshape(own.shape)
    pl.semaphore_wait(barrier, line - 1 + 2 + num_shot_devices - 1)

    sent = []

    def send(m, src, t, target, sem, cond=None):
        def copy():
            return pltpu.make_async_remote_copy(
                src_ref=own.at[m, t] if src == (0, "a") else slot(m, ids[src], t),
                dst_ref=slot(m, ids[src], t),
                send_sem=sem(),
                recv_sem=recv_sem.at[m * flags + ids[src] * 2 + t],
                device_id={"probe": ids[target]},
                device_id_type=MESH,
            )

        copy().start()
        sent.append((copy, cond))

    def arrive(m, src, t):
        pltpu.make_async_remote_copy(
            src_ref=slot(m, ids[src], t),
            dst_ref=slot(m, ids[src], t),
            send_sem=send_sem.at[m * flags + ids[src] * 2 + t],
            recv_sem=recv_sem.at[m * flags + ids[src] * 2 + t],
            device_id={"probe": ids[0, "right"]},
            device_id_type=MESH,
        ).wait_recv()

    def ring(m, src, t, name, cond=None):
        lane = 0 if name == "right" else 1
        send(
            m,
            src,
            t,
            (0, name),
            lambda: send_sem.at[(lane * members + m) * flags + ids[src] * 2 + t],
            cond,
        )

    def spread(m, src, cond=None):
        for t in (0, 1):
            ring(m, src, t, "right", cond)
            ring(m, src, 1 - t, "left", cond)

    def begin(m):
        for t in range(2):
            own_copy(m, t).start()
        for k in range(1, line):
            for dz in (k, -k):

                @pl.when(exists[dz])
                def _(dz=dz):
                    for t in (0, 1):
                        index = ((dz + line - 1) * members + m) * 2 + t
                        send(m, (0, "a"), t, (dz, "a"), lambda index=index: line_sem.at[index], exists[dz])

        spread(m, (0, "a"))

    def column(m, k):
        for dz, here in sides(k):

            @pl.when(here)
            def _(dz=dz, here=here):
                for t in (0, 1):
                    arrive(m, (dz, "a"), t)
                spread(m, (dz, "a"), here)

    def sides(k):
        if k == 0:
            return ((0, None),)
        return ((-k, exists[-k]), (k, exists[k]))

    def guarded(cond, fun):
        if cond is None:
            fun()
        else:
            pl.when(cond)(fun)

    def relay(m, k):
        for dz, cond in sides(k):

            def run(dz=dz, cond=cond):
                arrive(m, (dz, "left"), 0)
                ring(m, (dz, "left"), 0, "right", cond)
                arrive(m, (dz, "right"), 1)
                ring(m, (dz, "right"), 1, "left", cond)

            guarded(cond, run)

    def finish(m, k):
        for dz, cond in sides(k):

            def run(dz=dz):
                arrive(m, (dz, "left"), 1)
                arrive(m, (dz, "right"), 0)
                arrive(m, (dz, "far"), 0)
                arrive(m, (dz, "far"), 1)

            guarded(cond, run)

    def gather_steps(m):
        plan = []
        for k in range(1, line):
            plan.append(lambda k=k: column(m, k))
        for k in range(line):
            plan.append(lambda k=k: relay(m, k))
        return plan

    def gather_end(m):
        for k in range(line):
            finish(m, k)
        for t in range(2):
            own_copy(m, t).wait()

    for m in range(members):
        begin(m)

    row_in_tile = lax.broadcasted_iota(jnp.int32, (SUB, LANE), 0)
    lane_index = lax.broadcasted_iota(jnp.int32, (SUB, LANE), 1)
    at_first = lane_index == 0
    at_last = lane_index == LANE - 1

    def parity_of(rows):
        count = jnp.zeros((SUB, LANE), jnp.int32)
        for b in range(1, bounds_ref.shape[0] - 1):
            count = count + jnp.where(rows >= bounds_ref[b], 1, 0)
        return count % 2

    def prepare_sources():
        shots = wavelet_ref.shape[1]
        spacing = width // shots
        k = lax.broadcasted_iota(jnp.int32, (shots, width), 0)
        position = k * width // shots + spacing // 2
        index = lax.broadcasted_iota(jnp.int32, (shots, width), 1)
        onehot = jnp.where(position == groups * (index % LANE) + index // LANE, 1.0, 0.0)
        for m in range(members):
            amplitude = encodings_ref[m : m + 1, :].astype(jnp.float32) * wavelet_ref[...]
            source[m, 0:steps, :] = jnp.dot(
                amplitude,
                onehot,
                precision=lax.Precision.HIGHEST,
                preferred_element_type=jnp.float32,
            )

    def by_block(first, last, run):
        def body(b, carry):
            run(pl.multiple_of(b * block, block))
            return carry

        lax.fori_loop(first, last, body, 0)

    def flat(x):
        return x.reshape(rows_of_block, width)

    def tiled(x):
        return x.reshape(block, SUB, width)

    def prepare_coefficient(j):
        at = pl.ds(j, block)
        value = tiled(shuffle(flat(coefficient_in[at]), spread_table))
        coef[at] = value
        centre[at] = 2.0 - 4.0 * value

    def prepare_weight(j):
        at = pl.ds(j, block)
        seen = tiled(shuffle(flat(receiver_in[at]), spread_table))
        weight[at] = coef[at] * (seen * seen)

    def prepare_vectors(j):
        at = pl.ds(j, block)
        rows = []
        for i in range(block):
            parity = parity_of(row_in_tile * tiles + (j + i))
            parity_in[j + i] = parity
            rows.append(
                jnp.concatenate(
                    [
                        jnp.where(parity == 0, probes_in[0, j + i, :, c], probes_in[1, j + i, :, c])
                        for c in cols
                    ],
                    axis=1,
                )
            )
        both = tiled(shuffle(jnp.concatenate(rows, axis=0), spread_table))
        vec[2, at] = both
        for i in range(block):
            even = parity_in[j + i] == 0
            for c in cols:
                value = vec[2, j + i, :, c]
                vec[0, j + i, :, c] = jnp.where(even, value, 0.0)
                vec[1, j + i, :, c] = jnp.where(even, 0.0, value)

    def prepare_out():
        def body(i, carry):
            row = shot * out_rows + (row_in_tile % share) * tiles + (row_in_tile // share) * part_tiles + i
            parity_out[i] = parity_of(row)
            for c in cols:
                inverse[i, :, c] = 1.0 / inverse[i, :, c]
            return carry

        lax.fori_loop(0, part_tiles, body, 0)

    def halo(field):
        for c in cols:
            above = pltpu.roll(field[tiles, :, c], 1, 0)
            field[0, :, c] = jnp.where(row_in_tile == 0, 0.0, above)
            below = pltpu.roll(field[1, :, c], SUB - 1, 0)
            field[tiles + 1, :, c] = jnp.where(row_in_tile == SUB - 1, 0.0, below)

    def advance(field, before, j):
        here = [field[j + 1, :, c] for c in cols]
        west = [jnp.where(at_first, 0.0, pltpu.roll(here[-1], 1, 1))] + here[:-1]
        east = here[1:] + [jnp.where(at_last, 0.0, pltpu.roll(here[0], LANE - 1, 1))]
        moved = []
        for i, c in enumerate(cols):
            near = (field[j, :, c] + field[j + 2, :, c]) + (west[i] + east[i])
            value = centre[j, :, c] * here[i] + coef[j, :, c] * near
            if before is not None:
                value = value - before(j, c)
            moved.append(value)
        return moved

    def inner(field):
        return lambda j, c: field[j + 1, :, c]

    def sweep(body):
        def run(j, carry):
            body(j)
            return carry

        lax.fori_loop(0, tiles, run, 0, unroll=UNROLL)

    pair = range(num_probes)

    def start_fields(m):
        def body(j):
            for c in cols:
                value = u0[m, j + 1, :, c]
                for p in pair:
                    d1[p, j + 1, :, c] = vec[p, j, :, c] * value

        sweep(body)
        halo(u0.at[m])
        for p in pair:
            halo(d1.at[p])

    def levels_step(m, t):
        field = (u0.at[m], u1, u2)[t]
        before = (lambda j, c: um[m, j, :, c], inner(u0.at[m]), inner(u1))[t]
        result = (u1, u2, u3)[t]

        def body(j):
            for c, value in zip(cols, advance(field, before, j)):
                result[j + 1, :, c] = value

        sweep(body)
        for c in cols:
            row = jnp.broadcast_to(source[m, t : t + 1, c], (SUB, LANE))
            result[1, :, c] = result[1, :, c] + jnp.where(row_in_tile == SUB // 2, row, 0.0)
        if t < 2:
            halo(result)

    def chosen(j, values, i):
        return jnp.where(parity_in[j] == 1, values[0][i], values[1][i])

    def forward(m, t):
        level = (u1, u2, u3)[t]
        delta = (d1, d2, d3)[t]
        delta_before = (None, d1, d2)[t]
        delta_next = (d2, d3, e4)[t]

        def body(j):
            values = []
            for p in pair:
                prior = None if delta_before is None else inner(delta_before.at[p])
                step = advance(delta.at[p], prior, j)
                for i, c in enumerate(cols):
                    step[i] = step[i] + vec[p, j, :, c] * level[j + 1, :, c]
                    if t == 2:
                        step[i] = weight[j, :, c] * step[i]
                    delta_next[p, j + 1, :, c] = step[i]
                values.append(step)
            if t == 2:
                for i, c in enumerate(cols):
                    gain = level[j + 1, :, c] * chosen(j, values, i)
                    if m:
                        gain = total[j, :, c] + gain
                    total[j, :, c] = gain

        sweep(body)
        for p in pair:
            halo(delta_next.at[p])

    def adjoint(m, t):
        field = (e4, e3, e2)[t]
        before = (None, e4, e3)[t]
        result = (e3, e2, None)[t]
        delta = (d3, d2, d1)[t]
        level = (u2, u1, u0.at[m])[t]

        def body(j):
            values = []
            for p in pair:
                prior = None if before is None else inner(before.at[p])
                step = advance(field.at[p], prior, j)
                for i, c in enumerate(cols):
                    step[i] = step[i] + weight[j, :, c] * delta[p, j + 1, :, c]
                    if result is not None:
                        result[p, j + 1, :, c] = step[i]
                values.append(step)
            for i, c in enumerate(cols):
                total[j, :, c] = total[j, :, c] + level[j + 1, :, c] * chosen(j, values, i)

        sweep(body)
        if result is not None:
            for p in pair:
                halo(result.at[p])

    def piece(k, device):
        first = pl.multiple_of(device * share, share)
        return total.at[pl.ds(k * part_tiles, part_tiles), pl.ds(first, share), :]

    def pack():
        return [
            pltpu.make_async_copy(piece(k, shot), packed.at[:, pl.ds(k * share, share), :], pack_sem.at[k])
            for k in range(num_shot_devices)
        ]

    def swap():
        copies = []
        for away in range(1, num_shot_devices):
            other = (shot + away) % num_shot_devices
            for k in range(num_shot_devices):
                copies.append(
                    pltpu.make_async_remote_copy(
                        src_ref=piece(k, other),
                        dst_ref=partial.at[away - 1, :, pl.ds(k * share, share), :],
                        send_sem=swap_send.at[away - 1, k],
                        recv_sem=swap_recv.at[away - 1, k],
                        device_id={"shot": other},
                        device_id_type=MESH,
                    )
                )
        return copies

    def combine(j):
        at = pl.ds(j, block)
        value = packed[at]
        for away in range(1, num_shot_devices):
            value = value + partial[away - 1, at]
        value = tiled(shuffle(flat(value), collect_table)) * inverse[at]
        for p in pair:
            for i in range(block):
                keep = parity_out[j + i] != p % 2
                for n, c in enumerate(cols):
                    piece_of = value[i, :, n * LANE : (n + 1) * LANE] - coarse_in[p, j + i, :, c]
                    result_out[p, j + i, :, c] = jnp.where(keep, piece_of, 0.0)

    def deliver():
        copies = []
        for p in pair:
            for k in range(num_shot_devices):
                for e in range(share):
                    copies.append(
                        pltpu.make_async_copy(
                            result_out.at[p, :, k * share + e, :],
                            out_hbm.at[p, pl.ds(e * tiles + k * part_tiles, part_tiles), :],
                            out_sem.at[(p * num_shot_devices + k) * share + e],
                        )
                    )
        return copies

    blocks = tiles // block
    half = blocks // 2
    work = []

    def vectors_work():
        for load in load_probes:
            load.wait()
        by_block(0, blocks, prepare_vectors)

    def coefficient_work():
        for load in load_coefficient:
            load.wait()
        by_block(0, blocks, prepare_coefficient)

    def weight_work():
        for load in load_receiver:
            load.wait()
        by_block(0, blocks, prepare_weight)

    def out_work():
        for load in load_out:
            load.wait()
        prepare_out()

    work = [prepare_sources, coefficient_work, weight_work, vectors_work, out_work]
    for step in gather_steps(0):
        step()
        if work:
            work.pop(0)()
    for rest in work:
        rest()
    for m in range(members):
        plan = gather_steps(m + 1) if m + 1 < members else []
        if plan:
            for _ in range(line - 1):
                plan.pop(0)()
        gather_end(m)
        stages = [lambda: start_fields(m)]
        stages += [lambda t=t: levels_step(m, t) for t in range(3)]
        stages += [lambda t=t: forward(m, t) for t in range(3)]
        stages += [lambda t=t: adjoint(m, t) for t in range(3)]
        for stage in stages:
            stage()
            if plan:
                plan.pop(0)()
        for step in plan:
            step()
    copies = swap()
    packs = pack()
    for copy in copies + packs:
        copy.start()
    for copy in packs:
        copy.wait()
    for copy in copies:
        copy.wait_recv()
    by_block(0, part_tiles // block, combine)
    outs = deliver()
    for copy in outs:
        copy.start()
    for copy in copies:
        copy.wait_send()
    for copy, cond in sent:
        guarded(cond, lambda copy=copy: copy().wait_send())
    for copy in outs:
        copy.wait()


def on_device(
    num_shot_devices,
    num_probe_devices,
    probes,
    coarse_sample,
    coefficient,
    receiver,
    checkpoints,
    encodings,
    wavelet,
    bounds,
):
    members, levels, chunk, width = checkpoints.shape
    num_probes, num_rows, _ = probes.shape
    out_rows = coarse_sample.shape[1]
    tiles = num_rows // SUB
    line = num_probe_devices // INNER
    f32 = jnp.float32

    share = SUB // num_shot_devices
    part_tiles = tiles // num_shot_devices

    def plain(*lead):
        return pltpu.VMEM((*lead, tiles, SUB, width), f32)

    def ringed(*lead):
        return pltpu.VMEM((*lead, tiles + 2, SUB, width), f32)

    def part(*lead):
        return pltpu.VMEM((*lead, part_tiles, SUB, width), f32)

    others = num_shot_devices - 1
    anywhere = pl.BlockSpec(memory_space=pl.ANY)
    vmem = pl.BlockSpec(memory_space=pltpu.VMEM)
    loads = 1 + (num_probes + 2) * SUB + (1 + num_probes) * SUB
    return pl.pallas_call(
        functools.partial(kernel, num_shot_devices, num_probe_devices),
        out_shape=jax.ShapeDtypeStruct(coarse_sample.shape, f32),
        in_specs=[pl.BlockSpec(memory_space=pltpu.SMEM), vmem, vmem] + [anywhere] * 5,
        out_specs=anywhere,
        scratch_shapes=[
            pltpu.VMEM(checkpoints.shape, f32),
            pltpu.VMEM(checkpoints.shape, f32),
            plain(num_probes),
            part(num_probes),
            plain(),
            plain(),
            part(),
            pltpu.VMEM((width, width), jnp.bfloat16),
            pltpu.VMEM((width, width), jnp.bfloat16),
            pltpu.VMEM((tiles, SUB, LANE), jnp.int32),
            pltpu.VMEM((part_tiles, SUB, LANE), jnp.int32),
            plain(),
            plain(),
            plain(),
            plain(num_probes + 1),
            plain(members),
            ringed(members),
            ringed(),
            ringed(),
            ringed(),
            ringed(num_probes),
            ringed(num_probes),
            ringed(num_probes),
            ringed(num_probes),
            ringed(num_probes),
            ringed(num_probes),
            plain(),
            part(),
            part(others),
            part(num_probes),
            pltpu.VMEM((members, SUB, width), f32),
            pltpu.SemaphoreType.DMA((loads,)),
            pltpu.SemaphoreType.DMA((members * levels,)),
            pltpu.SemaphoreType.DMA((members * num_probe_devices * levels,)),
            pltpu.SemaphoreType.DMA((2 * members * num_probe_devices * levels,)),
            pltpu.SemaphoreType.DMA(((2 * line - 1) * members * levels,)),
            pltpu.SemaphoreType.DMA((num_shot_devices,)),
            pltpu.SemaphoreType.DMA((num_probes * SUB,)),
            pltpu.SemaphoreType.DMA((others, num_shot_devices)),
            pltpu.SemaphoreType.DMA((others, num_shot_devices)),
        ],
        compiler_params=pltpu.CompilerParams(
            collective_id=0, has_side_effects=True, vmem_limit_bytes=60 * 1024 * 1024
        ),
    )(
        bounds,
        encodings,
        wavelet,
        probes,
        coarse_sample,
        coefficient,
        receiver,
        checkpoints,
    )


def solution(mesh):
    return jax.shard_map(
        functools.partial(on_device, mesh.shape["shot"], mesh.shape["probe"]),
        mesh=mesh,
        in_specs=(
            P("probe", None, None),
            P("probe", "shot", None),
            P(),
            P(),
            P("shot", None, "probe", None),
            P("shot", None),
            P(),
            P(),
        ),
        out_specs=P("probe", "shot", None),
        check_vma=False,
    )
```

time: 51.1 us -> 47.8 us (0.935)
  Pallas kernels: 49 us -> 45.7 us
    pallas_call x1, Pallas kernels: 49 us -> 45.7 us  [on_device(): pl.pallas_call(functools.partial(kernel, num_shot_devices, num_probe_devi...]
where the time goes in v1:
time: 47.8 us; the launch traced here: 47.5 us
  Pallas kernels  45.7 us (96%)
  local copies, waits for them, and re-layouts  1.87 us (4%)
    pallas_call x1, Pallas kernels, on_device(): pl.pallas_call(functools.partial(kernel, num_shot_devices, num_probe_devi...  45.7 us
    unnamed x1, local copies, waits for them, and re-layouts  1.87 us

profile of v1, /device:TPU:1, one launch (start us, length us, event | category | flops | bytes accessed | tf_op | source)
XLA Modules:
  0.0 47.5 jit_solution(10763343360061259225)
XLA Ops:
  0.0 45.7 %shard_map.82 = f32[2,128,512]{2,1,0:T(8,128)} custom-call(s32[33]{0:T(128)} %bounds_ref.1, s32[2,256]{1,0:T(2,128)} %encodings_ref.1, f32[3,256]{1,0:T(4,128)} %wavelet_ref.1, f32[2,256,512]{2,1,0:T(8,128)} %probes_hbm.1, f32[2,128,512]{2,1,0:T(8,128)} %coarse_hbm.1, f32[256,512]{1,0:T(8,128)} %coefficient_hbm.1, f32[256,512]{1,0:T(8,128)} %receiver_hbm.1, ...), custom_call_target="tpu_custom_call" | custom-call | tf_op jit(solution)/shard_map/pallas_call | solution.py:673
  45.7 1.9 %copy.10 = f32[2,128,512]{2,1,0:T(8,128)} copy(f32[2,128,512]{2,1,0:T(8,128)} %shard_map.82) | data formatting | bytes 1048576

commit v2 on v1

--- a/solution.py
+++ b/solution.py
@@ -11,7 +11,8 @@
 SUB = 8
 LANE = 128
 INNER = 4
-UNROLL = 4
+UNROLL = 16
+BY_LINE = ()
 
 
 def kernel(
@@ -41,8 +42,8 @@
     centre,
     weight,
     vec,
-    um,
-    u0,
+    lev,
+    counter,
     u1,
     u2,
     u3,
@@ -59,9 +60,9 @@
     source,
     load_sem,
     own_sem,
-    recv_sem,
+    hop_sem,
+    far_sem,
     send_sem,
-    line_sem,
     pack_sem,
     out_sem,
     swap_send,
@@ -75,7 +76,6 @@
     cols = [pl.ds(c * LANE, LANE) for c in range(groups)]
     steps = wavelet_ref.shape[0]
     line = num_probe_devices // INNER
-    flags = num_probe_devices * 2
     share = SUB // num_shot_devices
     part_tiles = tiles // num_shot_devices
     block = min(8, part_tiles)
@@ -96,59 +96,15 @@
         for name, place in places.items()
     }
     exists = {dz: (z + dz >= 0) & (z + dz < line) for dz in range(1 - line, line)}
-    def slot(m, src, t):
+    def slot(m, src, t=None):
         first = src * chunk
-        sub = first // tiles
-        tile = first % tiles
-        if t:
-            return u0.at[m, pl.ds(tile + 1, chunk), sub, :]
-        return um.at[m, pl.ds(tile, chunk), sub, :]
-
-    def own_copy(m, t):
-        return pltpu.make_async_copy(own.at[m, t], slot(m, mine, t), own_sem.at[m * 2 + t])
-
-    load_own = pltpu.make_async_copy(checkpoints_hbm, own_in, load_sem.at[0])
+        rows = pl.ds(first % tiles + 1, chunk)
+        if t is None:
+            return lev.at[m, :, rows, first // tiles, :]
+        return lev.at[m, t, rows, first // tiles, :]
+
+    load_own = pltpu.make_async_copy(checkpoints_hbm, own_in, own_sem.at[0])
     load_own.start()
-
-    def strided_load(src, dst, base):
-        return [
-            pltpu.make_async_copy(src.at[pl.ds(k * tiles, tiles), :], dst.at[:, k, :], load_sem.at[base + k])
-            for k in range(SUB)
-        ]
-
-    load_probes = [
-        copy
-        for p in range(num_probes)
-        for copy in strided_load(probes_hbm.at[p], probes_in.at[p], 1 + p * SUB)
-    ]
-    base = 1 + num_probes * SUB
-    load_coefficient = strided_load(coefficient_hbm, coefficient_in, base)
-    load_receiver = strided_load(receiver_hbm, receiver_in, base + SUB)
-    base = base + 2 * SUB
-    load_out = []
-    for k in range(num_shot_devices):
-        for e in range(share):
-            first = pl.multiple_of(e * tiles + k * part_tiles, SUB)
-            near = pl.multiple_of(shot * out_rows + e * tiles + k * part_tiles, SUB)
-            load_out.append(
-                pltpu.make_async_copy(
-                    coefficient_hbm.at[pl.ds(near, part_tiles), :],
-                    inverse.at[:, k * share + e, :],
-                    load_sem.at[base],
-                )
-            )
-            base += 1
-            for p in range(num_probes):
-                load_out.append(
-                    pltpu.make_async_copy(
-                        coarse_hbm.at[p, pl.ds(first, part_tiles), :],
-                        coarse_in.at[p, :, k * share + e, :],
-                        load_sem.at[base],
-                    )
-                )
-                base += 1
-    for load in load_probes + load_coefficient + load_receiver + load_out:
-        load.start()
 
     barrier = pltpu.get_barrier_semaphore()
 
@@ -168,15 +124,14 @@
     for away in range(1, num_shot_devices):
         greet({"shot": (shot + away) % num_shot_devices})
 
-    def build_tables():
+    def build_table(table, spread):
         def body(b, carry):
             rows = pl.ds(pl.multiple_of(b * LANE, LANE), LANE)
             row = lax.broadcasted_iota(jnp.int32, (LANE, width), 0) + b * LANE
             col = lax.broadcasted_iota(jnp.int32, (LANE, width), 1)
-            place = groups * (col % LANE) + col // LANE
-            spread_table[rows, :] = jnp.where(row == place, 1.0, 0.0).astype(jnp.bfloat16)
-            place = groups * (row % LANE) + row // LANE
-            collect_table[rows, :] = jnp.where(col == place, 1.0, 0.0).astype(jnp.bfloat16)
+            fine, place = (row, col) if spread else (col, row)
+            match = fine == groups * (place % LANE) + place // LANE
+            table[rows, :] = jnp.where(match, 1.0, 0.0).astype(jnp.bfloat16)
             return carry
 
         lax.fori_loop(0, groups, body, 0)
@@ -192,81 +147,24 @@
         ]
         return moved[0] + (moved[1] + moved[2])
 
-    build_tables()
+    build_table(spread_table, True)
     load_own.wait()
     count = members * levels * chunk
     own[...] = shuffle(own_in[...].reshape(count, width), spread_table).reshape(own.shape)
     pl.semaphore_wait(barrier, line - 1 + 2 + num_shot_devices - 1)
 
-    sent = []
-
-    def send(m, src, t, target, sem, cond=None):
-        def copy():
-            return pltpu.make_async_remote_copy(
-                src_ref=own.at[m, t] if src == (0, "a") else slot(m, ids[src], t),
-                dst_ref=slot(m, ids[src], t),
-                send_sem=sem(),
-                recv_sem=recv_sem.at[m * flags + ids[src] * 2 + t],
-                device_id={"probe": ids[target]},
-                device_id_type=MESH,
-            )
-
-        copy().start()
-        sent.append((copy, cond))
-
-    def arrive(m, src, t):
+    def send(source, target, place, sem, which=0):
         pltpu.make_async_remote_copy(
-            src_ref=slot(m, ids[src], t),
-            dst_ref=slot(m, ids[src], t),
-            send_sem=send_sem.at[m * flags + ids[src] * 2 + t],
-            recv_sem=recv_sem.at[m * flags + ids[src] * 2 + t],
-            device_id={"probe": ids[0, "right"]},
+            src_ref=source,
+            dst_ref=place,
+            send_sem=send_sem.at[which],
+            recv_sem=sem,
+            device_id={"probe": ids[target]},
             device_id_type=MESH,
-        ).wait_recv()
-
-    def ring(m, src, t, name, cond=None):
-        lane = 0 if name == "right" else 1
-        send(
-            m,
-            src,
-            t,
-            (0, name),
-            lambda: send_sem.at[(lane * members + m) * flags + ids[src] * 2 + t],
-            cond,
-        )
-
-    def spread(m, src, cond=None):
-        for t in (0, 1):
-            ring(m, src, t, "right", cond)
-            ring(m, src, 1 - t, "left", cond)
-
-    def begin(m):
-        for t in range(2):
-            own_copy(m, t).start()
-        for k in range(1, line):
-            for dz in (k, -k):
-
-                @pl.when(exists[dz])
-                def _(dz=dz):
-                    for t in (0, 1):
-                        index = ((dz + line - 1) * members + m) * 2 + t
-                        send(m, (0, "a"), t, (dz, "a"), lambda index=index: line_sem.at[index], exists[dz])
-
-        spread(m, (0, "a"))
-
-    def column(m, k):
-        for dz, here in sides(k):
-
-            @pl.when(here)
-            def _(dz=dz, here=here):
-                for t in (0, 1):
-                    arrive(m, (dz, "a"), t)
-                spread(m, (dz, "a"), here)
-
-    def sides(k):
-        if k == 0:
-            return ((0, None),)
-        return ((-k, exists[-k]), (k, exists[k]))
+        ).start()
+
+    def await_bytes(ref, sem):
+        pltpu.make_async_copy(ref, ref, sem).wait()
 
     def guarded(cond, fun):
         if cond is None:
@@ -274,44 +172,113 @@
         else:
             pl.when(cond)(fun)
 
+    def sides(k):
+        if k == 0:
+            return ((0, None),)
+        return ((-k, exists[-k]), (k, exists[k]))
+
+    def own_to_place(m):
+        return pltpu.make_async_copy(own.at[m], slot(m, mine), own_sem.at[1 + m])
+
+    def along_line(m, kind, name, source, dz, ways):
+        place = slot(m, ids[dz, name])
+        for way in ways:
+            pl.when(exists[way])(
+                lambda way=way: send(source, (way, "a"), place, hop_sem.at[m, kind, z + dz], 1)
+            )
+
+    def to_ring(m, dz):
+        source = own.at[m] if dz == 0 else slot(m, ids[dz, "a"])
+        place = slot(m, ids[dz, "a"])
+        send(source, (0, "right"), place, hop_sem.at[m, 1, z + dz])
+        send(source, (0, "left"), place, hop_sem.at[m, 2, z + dz])
+
+    def own_line(m):
+        along_line(m, 0, "a", own.at[m], 0, (1, -1))
+
+    def own_ring(m):
+        to_ring(m, 0)
+
+    def passing(m, kind, name, k, after):
+        for dz, cond in sides(k):
+
+            def run(dz=dz):
+                place = slot(m, ids[dz, name])
+                await_bytes(place, hop_sem.at[m, kind, z + dz])
+                if k == 0:
+                    along_line(m, kind, name, place, 0, (1, -1))
+                elif k < line - 1:
+                    along_line(m, kind, name, place, dz, (1,) if dz < 0 else (-1,))
+                after(dz)
+
+            guarded(cond, run)
+
+    def column(m, k):
+        passing(m, 0, "a", k, lambda dz: to_ring(m, dz))
+
+    def across(m, k):
+        passing(m, 3, "far", k, lambda dz: None)
+
     def relay(m, k):
         for dz, cond in sides(k):
 
-            def run(dz=dz, cond=cond):
-                arrive(m, (dz, "left"), 0)
-                ring(m, (dz, "left"), 0, "right", cond)
-                arrive(m, (dz, "right"), 1)
-                ring(m, (dz, "right"), 1, "left", cond)
+            def run(dz=dz):
+                last = hop_sem.at[m, 3, z] if m in BY_LINE else far_sem.at[m]
+                await_bytes(slot(m, ids[dz, "left"]), hop_sem.at[m, 1, z + dz])
+                if k == 0 or m not in BY_LINE:
+                    place = slot(m, ids[dz, "left"], 0)
+                    send(place, (0, "right"), place, last)
+                await_bytes(slot(m, ids[dz, "right"]), hop_sem.at[m, 2, z + dz])
+                if k == 0 or m not in BY_LINE:
+                    place = slot(m, ids[dz, "right"], 1)
+                    send(place, (0, "left"), place, last)
 
             guarded(cond, run)
 
-    def finish(m, k):
-        for dz, cond in sides(k):
-
-            def run(dz=dz):
-                arrive(m, (dz, "left"), 1)
-                arrive(m, (dz, "right"), 0)
-                arrive(m, (dz, "far"), 0)
-                arrive(m, (dz, "far"), 1)
-
-            guarded(cond, run)
-
-    def gather_steps(m):
-        plan = []
-        for k in range(1, line):
-            plan.append(lambda k=k: column(m, k))
-        for k in range(line):
-            plan.append(lambda k=k: relay(m, k))
-        return plan
-
     def gather_end(m):
-        for k in range(line):
-            finish(m, k)
-        for t in range(2):
-            own_copy(m, t).wait()
+        if m not in BY_LINE:
+            await_bytes(counter.at[pl.ds(0, line)], far_sem.at[m])
+        own_to_place(m).wait()
+
+    def sends_end():
+        await_bytes(counter, send_sem.at[0])
+        for m in range(members):
+            for dz in (1, -1):
+                for _ in range(2 if m in BY_LINE else 1):
+                    for k in range(line - 1):
+                        cond = exists[dz] if k == 0 else exists[dz] & exists[-k * dz]
+                        pl.when(cond)(lambda: await_bytes(own.at[0], send_sem.at[1]))
 
     for m in range(members):
-        begin(m)
+        own_line(m)
+    own_ring(0)
+    for m in range(members):
+        own_to_place(m).start()
+
+    def strided_load(src, dst, sem):
+        for k in range(SUB):
+            pltpu.make_async_copy(src.at[pl.ds(k * tiles, tiles), :], dst.at[:, k, :], sem).start()
+
+    strided_load(coefficient_hbm, coefficient_in, load_sem.at[0])
+    strided_load(receiver_hbm, receiver_in, load_sem.at[1])
+    for p in range(num_probes):
+        strided_load(probes_hbm.at[p], probes_in.at[p], load_sem.at[2])
+    build_table(collect_table, False)
+    for k in range(num_shot_devices):
+        for e in range(share):
+            first = pl.multiple_of(e * tiles + k * part_tiles, SUB)
+            near = pl.multiple_of(shot * out_rows + e * tiles + k * part_tiles, SUB)
+            pltpu.make_async_copy(
+                coefficient_hbm.at[pl.ds(near, part_tiles), :],
+                inverse.at[:, k * share + e, :],
+                load_sem.at[3],
+            ).start()
+            for p in range(num_probes):
+                pltpu.make_async_copy(
+                    coarse_hbm.at[p, pl.ds(first, part_tiles), :],
+                    coarse_in.at[p, :, k * share + e, :],
+                    load_sem.at[4],
+                ).start()
 
     row_in_tile = lax.broadcasted_iota(jnp.int32, (SUB, LANE), 0)
     lane_index = lax.broadcasted_iota(jnp.int32, (SUB, LANE), 1)
@@ -396,7 +363,7 @@
                 inverse[i, :, c] = 1.0 / inverse[i, :, c]
             return carry
 
-        lax.fori_loop(0, part_tiles, body, 0)
+        lax.fori_loop(0, part_tiles, body, 0, unroll=4)
 
     def halo(field):
         for c in cols:
@@ -433,18 +400,18 @@
     def start_fields(m):
         def body(j):
             for c in cols:
-                value = u0[m, j + 1, :, c]
+                value = lev[m, 1, j + 1, :, c]
                 for p in pair:
                     d1[p, j + 1, :, c] = vec[p, j, :, c] * value
 
         sweep(body)
-        halo(u0.at[m])
+        halo(lev.at[m, 1])
         for p in pair:
             halo(d1.at[p])
 
     def levels_step(m, t):
-        field = (u0.at[m], u1, u2)[t]
-        before = (lambda j, c: um[m, j, :, c], inner(u0.at[m]), inner(u1))[t]
+        field = (lev.at[m, 1], u1, u2)[t]
+        before = (inner(lev.at[m, 0]), inner(lev.at[m, 1]), inner(u1))[t]
         result = (u1, u2, u3)[t]
 
         def body(j):
@@ -494,7 +461,7 @@
         before = (None, e4, e3)[t]
         result = (e3, e2, None)[t]
         delta = (d3, d2, d1)[t]
-        level = (u2, u1, u0.at[m])[t]
+        level = (u2, u1, lev.at[m, 1])[t]
 
         def body(j):
             values = []
@@ -518,28 +485,21 @@
         first = pl.multiple_of(device * share, share)
         return total.at[pl.ds(k * part_tiles, part_tiles), pl.ds(first, share), :]
 
-    def pack():
-        return [
-            pltpu.make_async_copy(piece(k, shot), packed.at[:, pl.ds(k * share, share), :], pack_sem.at[k])
-            for k in range(num_shot_devices)
-        ]
-
-    def swap():
-        copies = []
-        for away in range(1, num_shot_devices):
-            other = (shot + away) % num_shot_devices
-            for k in range(num_shot_devices):
-                copies.append(
-                    pltpu.make_async_remote_copy(
-                        src_ref=piece(k, other),
-                        dst_ref=partial.at[away - 1, :, pl.ds(k * share, share), :],
-                        send_sem=swap_send.at[away - 1, k],
-                        recv_sem=swap_recv.at[away - 1, k],
-                        device_id={"shot": other},
-                        device_id_type=MESH,
-                    )
-                )
-        return copies
+    def start_swap():
+        for k in range(num_shot_devices):
+            for away in range(1, num_shot_devices):
+                other = (shot + away) % num_shot_devices
+                pltpu.make_async_remote_copy(
+                    src_ref=piece(k, other),
+                    dst_ref=partial.at[away - 1, :, pl.ds(k * share, share), :],
+                    send_sem=swap_send.at[0],
+                    recv_sem=swap_recv.at[away - 1],
+                    device_id={"shot": other},
+                    device_id_type=MESH,
+                ).start()
+            pltpu.make_async_copy(
+                piece(k, shot), packed.at[:, pl.ds(k * share, share), :], pack_sem.at[0]
+            ).start()
 
     def combine(j):
         at = pl.ds(j, block)
@@ -554,57 +514,65 @@
                     piece_of = value[i, :, n * LANE : (n + 1) * LANE] - coarse_in[p, j + i, :, c]
                     result_out[p, j + i, :, c] = jnp.where(keep, piece_of, 0.0)
 
-    def deliver():
-        copies = []
-        for p in pair:
-            for k in range(num_shot_devices):
-                for e in range(share):
-                    copies.append(
-                        pltpu.make_async_copy(
-                            result_out.at[p, :, k * share + e, :],
-                            out_hbm.at[p, pl.ds(e * tiles + k * part_tiles, part_tiles), :],
-                            out_sem.at[(p * num_shot_devices + k) * share + e],
-                        )
-                    )
-        return copies
-
-    blocks = tiles // block
-    half = blocks // 2
+    def deliver(p):
+        for k in range(num_shot_devices):
+            for e in range(share):
+                pltpu.make_async_copy(
+                    result_out.at[p, :, k * share + e, :],
+                    out_hbm.at[p, pl.ds(e * tiles + k * part_tiles, part_tiles), :],
+                    out_sem.at[0],
+                ).start()
+
     work = []
 
-    def vectors_work():
-        for load in load_probes:
-            load.wait()
-        by_block(0, blocks, prepare_vectors)
-
-    def coefficient_work():
-        for load in load_coefficient:
-            load.wait()
-        by_block(0, blocks, prepare_coefficient)
-
-    def weight_work():
-        for load in load_receiver:
-            load.wait()
-        by_block(0, blocks, prepare_weight)
+    def add_work(run, ref=None, sem=None):
+        def first():
+            if ref is not None:
+                await_bytes(ref, sem)
+            run(0)
+
+        work.append(first)
+        for b in range(1, tiles // block):
+            work.append(lambda b=b: run(b * block))
+
+    work.append(prepare_sources)
+    add_work(prepare_coefficient, coefficient_in, load_sem.at[0])
+    add_work(prepare_weight, receiver_in, load_sem.at[1])
+    add_work(prepare_vectors, probes_in, load_sem.at[2])
 
     def out_work():
-        for load in load_out:
-            load.wait()
+        await_bytes(inverse, load_sem.at[3])
         prepare_out()
-
-    work = [prepare_sources, coefficient_work, weight_work, vectors_work, out_work]
-    for step in gather_steps(0):
+        await_bytes(coarse_in, load_sem.at[4])
+
+    work.append(out_work)
+    def gather_plan():
+        plan = []
+        for k in range(1, line):
+            for m in range(members):
+                plan.append(lambda k=k, m=m: column(m, k))
+                if k == 1 and m + 1 < members:
+                    plan.append(lambda m=m: own_ring(m + 1))
+        ends = []
+        for m in range(members):
+            last = [lambda k=k, m=m: relay(m, k) for k in range(line)]
+            if m in BY_LINE:
+                last = [f for k in range(line) for f in (last[k], lambda k=k, m=m: across(m, k))]
+            ends.append(last)
+        return plan + ends[0], ends[1:]
+
+    before, during = gather_plan()
+    per = -(-len(work) // len(before))
+    for step in before:
         step()
-        if work:
-            work.pop(0)()
+        for _ in range(per):
+            if work:
+                work.pop(0)()
     for rest in work:
         rest()
     for m in range(members):
-        plan = gather_steps(m + 1) if m + 1 < members else []
-        if plan:
-            for _ in range(line - 1):
-                plan.pop(0)()
         gather_end(m)
+        plan = during[m] if m < len(during) else []
         stages = [lambda: start_fields(m)]
         stages += [lambda t=t: levels_step(m, t) for t in range(3)]
         stages += [lambda t=t: forward(m, t) for t in range(3)]
@@ -615,24 +583,16 @@
                 plan.pop(0)()
         for step in plan:
             step()
-    copies = swap()
-    packs = pack()
-    for copy in copies + packs:
-        copy.start()
-    for copy in packs:
-        copy.wait()
-    for copy in copies:
-        copy.wait_recv()
+    start_swap()
+    await_bytes(packed, pack_sem.at[0])
+    for away in range(1, num_shot_devices):
+        await_bytes(partial.at[away - 1], swap_recv.at[away - 1])
     by_block(0, part_tiles // block, combine)
-    outs = deliver()
-    for copy in outs:
-        copy.start()
-    for copy in copies:
-        copy.wait_send()
-    for copy, cond in sent:
-        guarded(cond, lambda copy=copy: copy().wait_send())
-    for copy in outs:
-        copy.wait()
+    for p in pair:
+        deliver(p)
+    await_bytes(partial, swap_send.at[0])
+    sends_end()
+    await_bytes(result_out, out_sem.at[0])
 
 
 def on_device(
@@ -654,8 +614,8 @@
     line = num_probe_devices // INNER
     f32 = jnp.float32
 
-    share = SUB // num_shot_devices
     part_tiles = tiles // num_shot_devices
+    whole_pieces = sum(2 * line + (1 if m in BY_LINE else line) for m in range(members))
 
     def plain(*lead):
         return pltpu.VMEM((*lead, tiles, SUB, width), f32)
@@ -669,7 +629,6 @@
     others = num_shot_devices - 1
     anywhere = pl.BlockSpec(memory_space=pl.ANY)
     vmem = pl.BlockSpec(memory_space=pltpu.VMEM)
-    loads = 1 + (num_probes + 2) * SUB + (1 + num_probes) * SUB
     return pl.pallas_call(
         functools.partial(kernel, num_shot_devices, num_probe_devices),
         out_shape=jax.ShapeDtypeStruct(coarse_sample.shape, f32),
@@ -691,8 +650,8 @@
             plain(),
             plain(),
             plain(num_probes + 1),
-            plain(members),
-            ringed(members),
+            ringed(members, levels),
+            pltpu.VMEM((whole_pieces, levels, chunk, width), f32),
             ringed(),
             ringed(),
             ringed(),
@@ -707,15 +666,15 @@
             part(others),
             part(num_probes),
             pltpu.VMEM((members, SUB, width), f32),
-            pltpu.SemaphoreType.DMA((loads,)),
-            pltpu.SemaphoreType.DMA((members * levels,)),
-            pltpu.SemaphoreType.DMA((members * num_probe_devices * levels,)),
-            pltpu.SemaphoreType.DMA((2 * members * num_probe_devices * levels,)),
-            pltpu.SemaphoreType.DMA(((2 * line - 1) * members * levels,)),
-            pltpu.SemaphoreType.DMA((num_shot_devices,)),
-            pltpu.SemaphoreType.DMA((num_probes * SUB,)),
-            pltpu.SemaphoreType.DMA((others, num_shot_devices)),
-            pltpu.SemaphoreType.DMA((others, num_shot_devices)),
+            pltpu.SemaphoreType.DMA((5,)),
+            pltpu.SemaphoreType.DMA((1 + members,)),
+            pltpu.SemaphoreType.DMA((members, 4, line)),
+            pltpu.SemaphoreType.DMA((members,)),
+            pltpu.SemaphoreType.DMA((2,)),
+            pltpu.SemaphoreType.DMA((1,)),
+            pltpu.SemaphoreType.DMA((1,)),
+            pltpu.SemaphoreType.DMA((1,)),
+            pltpu.SemaphoreType.DMA((others,)),
         ],
         compiler_params=pltpu.CompilerParams(
             collective_id=0, has_side_effects=True, vmem_limit_bytes=60 * 1024 * 1024

time: 47.8 us -> 36.6 us (0.77)
  Pallas kernels: 45.7 us -> 34.5 us
    pallas_call x1, Pallas kernels: 45.7 us -> 34.5 us  [on_device(): pl.pallas_call(functools.partial(kernel, num_shot_devices, num_probe_devi...]
where the time goes in v2:
time: 36.6 us; the launch traced here: 36.4 us
  Pallas kernels  34.5 us (94%)
  local copies, waits for them, and re-layouts  1.87 us (5%)
    pallas_call x1, Pallas kernels, on_device(): pl.pallas_call(functools.partial(kernel, num_shot_devices, num_probe_devi...  34.5 us
    unnamed x1, local copies, waits for them, and re-layouts  1.87 us

profile of v2, /device:TPU:1, one launch (start us, length us, event | category | flops | bytes accessed | tf_op | source)
XLA Modules:
  0.0 36.4 jit_solution(16801164248614284372)
XLA Ops:
  0.0 34.5 %shard_map.82 = f32[2,128,512]{2,1,0:T(8,128)} custom-call(s32[33]{0:T(128)} %bounds_ref.1, s32[2,256]{1,0:T(2,128)} %encodings_ref.1, f32[3,256]{1,0:T(4,128)} %wavelet_ref.1, f32[2,256,512]{2,1,0:T(8,128)} %probes_hbm.1, f32[2,128,512]{2,1,0:T(8,128)} %coarse_hbm.1, f32[256,512]{1,0:T(8,128)} %coefficient_hbm.1, f32[256,512]{1,0:T(8,128)} %receiver_hbm.1, ...), custom_call_target="tpu_custom_call" | custom-call | tf_op jit(solution)/shard_map/pallas_call | solution.py:632
  34.5 1.9 %copy.10 = f32[2,128,512]{2,1,0:T(8,128)} copy(f32[2,128,512]{2,1,0:T(8,128)} %shard_map.82) | data formatting | bytes 1048576

commit v3 on v2

--- a/solution.py
+++ b/solution.py
@@ -11,8 +11,7 @@
 SUB = 8
 LANE = 128
 INNER = 4
-UNROLL = 16
-BY_LINE = ()
+UNROLL = 32
 
 
 def kernel(
@@ -78,6 +77,7 @@
     line = num_probe_devices // INNER
     share = SUB // num_shot_devices
     part_tiles = tiles // num_shot_devices
+    by_line = (members - 1,)
     block = min(8, part_tiles)
     rows_of_block = block * SUB
 
@@ -223,35 +223,36 @@
         for dz, cond in sides(k):
 
             def run(dz=dz):
-                last = hop_sem.at[m, 3, z] if m in BY_LINE else far_sem.at[m]
+                last = hop_sem.at[m, 3, z] if m in by_line else far_sem.at[m]
                 await_bytes(slot(m, ids[dz, "left"]), hop_sem.at[m, 1, z + dz])
-                if k == 0 or m not in BY_LINE:
+                if k == 0 or m not in by_line:
                     place = slot(m, ids[dz, "left"], 0)
                     send(place, (0, "right"), place, last)
                 await_bytes(slot(m, ids[dz, "right"]), hop_sem.at[m, 2, z + dz])
-                if k == 0 or m not in BY_LINE:
+                if k == 0 or m not in by_line:
                     place = slot(m, ids[dz, "right"], 1)
                     send(place, (0, "left"), place, last)
 
             guarded(cond, run)
 
     def gather_end(m):
-        if m not in BY_LINE:
+        if m not in by_line:
             await_bytes(counter.at[pl.ds(0, line)], far_sem.at[m])
         own_to_place(m).wait()
 
-    def sends_end():
-        await_bytes(counter, send_sem.at[0])
+    def line_sends_end():
         for m in range(members):
             for dz in (1, -1):
-                for _ in range(2 if m in BY_LINE else 1):
+                for _ in range(2 if m in by_line else 1):
                     for k in range(line - 1):
                         cond = exists[dz] if k == 0 else exists[dz] & exists[-k * dz]
                         pl.when(cond)(lambda: await_bytes(own.at[0], send_sem.at[1]))
 
+    own_line(0)
     for m in range(members):
+        own_ring(m)
+    for m in range(1, members):
         own_line(m)
-    own_ring(0)
     for m in range(members):
         own_to_place(m).start()
 
@@ -306,13 +307,6 @@
                 precision=lax.Precision.HIGHEST,
                 preferred_element_type=jnp.float32,
             )
-
-    def by_block(first, last, run):
-        def body(b, carry):
-            run(pl.multiple_of(b * block, block))
-            return carry
-
-        lax.fori_loop(first, last, body, 0)
 
     def flat(x):
         return x.reshape(rows_of_block, width)
@@ -388,12 +382,12 @@
     def inner(field):
         return lambda j, c: field[j + 1, :, c]
 
-    def sweep(body):
+    def sweep(body, first=0, last=tiles):
         def run(j, carry):
             body(j)
             return carry
 
-        lax.fori_loop(0, tiles, run, 0, unroll=UNROLL)
+        lax.fori_loop(first, last, run, 0, unroll=min(UNROLL, last - first))
 
     pair = range(num_probes)
 
@@ -447,10 +441,7 @@
                 values.append(step)
             if t == 2:
                 for i, c in enumerate(cols):
-                    gain = level[j + 1, :, c] * chosen(j, values, i)
-                    if m:
-                        gain = total[j, :, c] + gain
-                    total[j, :, c] = gain
+                    total[j, :, c] = total[j, :, c] + level[j + 1, :, c] * chosen(j, values, i)
 
         sweep(body)
         for p in pair:
@@ -476,7 +467,12 @@
             for i, c in enumerate(cols):
                 total[j, :, c] = total[j, :, c] + level[j + 1, :, c] * chosen(j, values, i)
 
-        sweep(body)
+        if result is None:
+            for k in range(num_shot_devices):
+                sweep(body, k * part_tiles, (k + 1) * part_tiles)
+                pl.when(m == members - 1)(lambda k=k: start_swap(k))
+        else:
+            sweep(body)
         if result is not None:
             for p in pair:
                 halo(result.at[p])
@@ -485,21 +481,20 @@
         first = pl.multiple_of(device * share, share)
         return total.at[pl.ds(k * part_tiles, part_tiles), pl.ds(first, share), :]
 
-    def start_swap():
-        for k in range(num_shot_devices):
-            for away in range(1, num_shot_devices):
-                other = (shot + away) % num_shot_devices
-                pltpu.make_async_remote_copy(
-                    src_ref=piece(k, other),
-                    dst_ref=partial.at[away - 1, :, pl.ds(k * share, share), :],
-                    send_sem=swap_send.at[0],
-                    recv_sem=swap_recv.at[away - 1],
-                    device_id={"shot": other},
-                    device_id_type=MESH,
-                ).start()
-            pltpu.make_async_copy(
-                piece(k, shot), packed.at[:, pl.ds(k * share, share), :], pack_sem.at[0]
+    def start_swap(k):
+        for away in range(1, num_shot_devices):
+            other = (shot + away) % num_shot_devices
+            pltpu.make_async_remote_copy(
+                src_ref=piece(k, other),
+                dst_ref=partial.at[away - 1, :, pl.ds(k * share, share), :],
+                send_sem=swap_send.at[0],
+                recv_sem=swap_recv.at[away - 1],
+                device_id={"shot": other},
+                device_id_type=MESH,
             ).start()
+        pltpu.make_async_copy(
+            piece(k, shot), packed.at[:, pl.ds(k * share, share), :], pack_sem.at[0]
+        ).start()
 
     def combine(j):
         at = pl.ds(j, block)
@@ -514,14 +509,16 @@
                     piece_of = value[i, :, n * LANE : (n + 1) * LANE] - coarse_in[p, j + i, :, c]
                     result_out[p, j + i, :, c] = jnp.where(keep, piece_of, 0.0)
 
-    def deliver(p):
-        for k in range(num_shot_devices):
-            for e in range(share):
-                pltpu.make_async_copy(
-                    result_out.at[p, :, k * share + e, :],
-                    out_hbm.at[p, pl.ds(e * tiles + k * part_tiles, part_tiles), :],
-                    out_sem.at[0],
-                ).start()
+    def deliver(j):
+        for p in pair:
+            for k in range(num_shot_devices):
+                for e in range(share):
+                    first = e * tiles + k * part_tiles + j
+                    pltpu.make_async_copy(
+                        result_out.at[p, pl.ds(j, block), k * share + e, :],
+                        out_hbm.at[p, pl.ds(first, block), :],
+                        out_sem.at[0],
+                    ).start()
 
     work = []
 
@@ -535,6 +532,10 @@
         for b in range(1, tiles // block):
             work.append(lambda b=b: run(b * block))
 
+    def clear_total():
+        total[...] = jnp.zeros_like(total)
+
+    work.append(clear_total)
     work.append(prepare_sources)
     add_work(prepare_coefficient, coefficient_in, load_sem.at[0])
     add_work(prepare_weight, receiver_in, load_sem.at[1])
@@ -545,53 +546,58 @@
         prepare_out()
         await_bytes(coarse_in, load_sem.at[4])
 
-    work.append(out_work)
+    work.insert(1, out_work)
     def gather_plan():
-        plan = []
-        for k in range(1, line):
-            for m in range(members):
-                plan.append(lambda k=k, m=m: column(m, k))
-                if k == 1 and m + 1 < members:
-                    plan.append(lambda m=m: own_ring(m + 1))
-        ends = []
-        for m in range(members):
-            last = [lambda k=k, m=m: relay(m, k) for k in range(line)]
-            if m in BY_LINE:
-                last = [f for k in range(line) for f in (last[k], lambda k=k, m=m: across(m, k))]
-            ends.append(last)
-        return plan + ends[0], ends[1:]
-
-    before, during = gather_plan()
-    per = -(-len(work) // len(before))
+        last = members - 1
+        plan = [lambda: column(0, 1), lambda: relay(last, 0)]
+        plan += [lambda: column(last, 1), lambda: relay(0, 0)]
+        for k in range(2, line):
+            plan += [lambda k=k: column(0, k), lambda k=k: across(last, k - 2)]
+            plan += [lambda k=k: column(last, k), lambda k=k: relay(0, k - 1)]
+        plan.append(lambda: relay(0, line - 1))
+        rest = [lambda: across(last, line - 1)]
+        rest += [lambda k=k: relay(last, k) for k in range(1, line)]
+        return plan, rest
+
+    before, after = gather_plan()
+    while len(work) > len(before):
+        work.pop(0)()
     for step in before:
         step()
-        for _ in range(per):
-            if work:
-                work.pop(0)()
+        if work:
+            work.pop(0)()
     for rest in work:
         rest()
-    for m in range(members):
+    def arrived(m):
+        if m == members - 1:
+            for step in after:
+                step()
+            line_sends_end()
         gather_end(m)
-        plan = during[m] if m < len(during) else []
-        stages = [lambda: start_fields(m)]
-        stages += [lambda t=t: levels_step(m, t) for t in range(3)]
-        stages += [lambda t=t: forward(m, t) for t in range(3)]
-        stages += [lambda t=t: adjoint(m, t) for t in range(3)]
-        for stage in stages:
-            stage()
-            if plan:
-                plan.pop(0)()
-        for step in plan:
-            step()
-    start_swap()
+        if m == 0:
+            across(members - 1, line - 2)
+
+    def member(m, carry):
+        for i in range(members):
+            pl.when(m == i)(lambda i=i: arrived(i))
+        start_fields(m)
+        for t in range(3):
+            levels_step(m, t)
+        for t in range(3):
+            forward(m, t)
+        for t in range(3):
+            adjoint(m, t)
+        return carry
+
+    lax.fori_loop(0, members, member, 0)
     await_bytes(packed, pack_sem.at[0])
     for away in range(1, num_shot_devices):
         await_bytes(partial.at[away - 1], swap_recv.at[away - 1])
-    by_block(0, part_tiles // block, combine)
-    for p in pair:
-        deliver(p)
+    for b in range(part_tiles // block):
+        combine(b * block)
+        deliver(b * block)
     await_bytes(partial, swap_send.at[0])
-    sends_end()
+    await_bytes(counter, send_sem.at[0])
     await_bytes(result_out, out_sem.at[0])
 
 
@@ -615,7 +621,7 @@
     f32 = jnp.float32
 
     part_tiles = tiles // num_shot_devices
-    whole_pieces = sum(2 * line + (1 if m in BY_LINE else line) for m in range(members))
+    whole_pieces = members * 3 * line - (line - 1)
 
     def plain(*lead):
         return pltpu.VMEM((*lead, tiles, SUB, width), f32)

time: 36.6 us -> 35.3 us (0.964)
  Pallas kernels: 34.5 us -> 33.2 us
    pallas_call x1, Pallas kernels: 34.5 us -> 33.2 us  [on_device(): pl.pallas_call(functools.partial(kernel, num_shot_devices, num_probe_devi...]
where the time goes in v3:
time: 35.3 us; the launch traced here: 35 us
  Pallas kernels  33.2 us (94%)
  local copies, waits for them, and re-layouts  1.87 us (5%)
    pallas_call x1, Pallas kernels, on_device(): pl.pallas_call(functools.partial(kernel, num_shot_devices, num_probe_devi...  33.2 us
    unnamed x1, local copies, waits for them, and re-layouts  1.87 us

profile of v3, /device:TPU:1, one launch (start us, length us, event | category | flops | bytes accessed | tf_op | source)
XLA Modules:
  0.0 35.0 jit_solution(16019222131826459516)
XLA Ops:
  0.0 33.2 %shard_map.82 = f32[2,128,512]{2,1,0:T(8,128)} custom-call(s32[33]{0:T(128)} %bounds_ref.1, s32[2,256]{1,0:T(2,128)} %encodings_ref.1, f32[3,256]{1,0:T(4,128)} %wavelet_ref.1, f32[2,256,512]{2,1,0:T(8,128)} %probes_hbm.1, f32[2,128,512]{2,1,0:T(8,128)} %coarse_hbm.1, f32[256,512]{1,0:T(8,128)} %coefficient_hbm.1, f32[256,512]{1,0:T(8,128)} %receiver_hbm.1, ...), custom_call_target="tpu_custom_call" | custom-call | tf_op jit(solution)/shard_map/pallas_call | solution.py:638
  33.2 1.9 %copy.10 = f32[2,128,512]{2,1,0:T(8,128)} copy(f32[2,128,512]{2,1,0:T(8,128)} %shard_map.82) | data formatting | bytes 1048576

commit v4 on v3

--- a/solution.py
+++ b/solution.py
@@ -180,64 +180,75 @@
     def own_to_place(m):
         return pltpu.make_async_copy(own.at[m], slot(m, mine), own_sem.at[1 + m])
 
-    def along_line(m, kind, name, source, dz, ways):
-        place = slot(m, ids[dz, name])
+    def along_line(m, t, kind, name, source, dz, ways):
+        place = slot(m, ids[dz, name], t)
+        sem = hop_sem.at[m, kind, z + dz, t or 0]
         for way in ways:
             pl.when(exists[way])(
-                lambda way=way: send(source, (way, "a"), place, hop_sem.at[m, kind, z + dz], 1)
+                lambda way=way: send(place if source is None else source, (way, "a"), place, sem, 1)
             )
 
-    def to_ring(m, dz):
-        source = own.at[m] if dz == 0 else slot(m, ids[dz, "a"])
-        place = slot(m, ids[dz, "a"])
-        send(source, (0, "right"), place, hop_sem.at[m, 1, z + dz])
-        send(source, (0, "left"), place, hop_sem.at[m, 2, z + dz])
+    def relayed(m, dz):
+        return dz == 0 or m not in by_line
+
+    def to_ring(m, dz, t):
+        source = own.at[m, t] if dz == 0 else slot(m, ids[dz, "a"], t)
+        place = slot(m, ids[dz, "a"], t)
+        for kind, name in ((1, "right"), (2, "left")):
+            passed_on = relayed(m, dz) and t == kind - 1
+            sem = hop_sem.at[m, kind, z + dz, 0] if passed_on else far_sem.at[m]
+            send(source, (0, name), place, sem)
 
     def own_line(m):
-        along_line(m, 0, "a", own.at[m], 0, (1, -1))
+        for t in range(levels):
+            along_line(m, t, 0, "a", own.at[m, t], 0, (1, -1))
 
     def own_ring(m):
-        to_ring(m, 0)
-
-    def passing(m, kind, name, k, after):
+        for t in range(levels):
+            to_ring(m, 0, t)
+
+    def onward(k, dz):
+        if k == 0:
+            return (1, -1)
+        if k < line - 1:
+            return (1,) if dz < 0 else (-1,)
+        return ()
+
+    def column(m, k):
+        for t in range(levels):
+            for dz, cond in sides(k):
+
+                def run(dz=dz, t=t):
+                    await_bytes(slot(m, ids[dz, "a"], t), hop_sem.at[m, 0, z + dz, t])
+                    along_line(m, t, 0, "a", None, dz, onward(k, dz))
+                    to_ring(m, dz, t)
+
+                guarded(cond, run)
+
+    def across(m, k):
         for dz, cond in sides(k):
 
             def run(dz=dz):
-                place = slot(m, ids[dz, name])
-                await_bytes(place, hop_sem.at[m, kind, z + dz])
-                if k == 0:
-                    along_line(m, kind, name, place, 0, (1, -1))
-                elif k < line - 1:
-                    along_line(m, kind, name, place, dz, (1,) if dz < 0 else (-1,))
-                after(dz)
+                await_bytes(slot(m, ids[dz, "far"]), hop_sem.at[m, 3, z + dz, 0])
+                along_line(m, None, 3, "far", None, dz, onward(k, dz))
 
             guarded(cond, run)
-
-    def column(m, k):
-        passing(m, 0, "a", k, lambda dz: to_ring(m, dz))
-
-    def across(m, k):
-        passing(m, 3, "far", k, lambda dz: None)
 
     def relay(m, k):
         for dz, cond in sides(k):
 
             def run(dz=dz):
-                last = hop_sem.at[m, 3, z] if m in by_line else far_sem.at[m]
-                await_bytes(slot(m, ids[dz, "left"]), hop_sem.at[m, 1, z + dz])
-                if k == 0 or m not in by_line:
-                    place = slot(m, ids[dz, "left"], 0)
-                    send(place, (0, "right"), place, last)
-                await_bytes(slot(m, ids[dz, "right"]), hop_sem.at[m, 2, z + dz])
-                if k == 0 or m not in by_line:
-                    place = slot(m, ids[dz, "right"], 1)
-                    send(place, (0, "left"), place, last)
+                last = hop_sem.at[m, 3, z, 0] if m in by_line else far_sem.at[m]
+                for t, (name, way) in enumerate((("left", "right"), ("right", "left"))):
+                    place = slot(m, ids[dz, name], t)
+                    await_bytes(place, hop_sem.at[m, 1 + t, z + dz, 0])
+                    send(place, (0, way), place, last)
 
             guarded(cond, run)
 
     def gather_end(m):
-        if m not in by_line:
-            await_bytes(counter.at[pl.ds(0, line)], far_sem.at[m])
+        pieces = 2 * line - 1 if m in by_line else 2 * line
+        await_bytes(counter.at[pl.ds(0, pieces)], far_sem.at[m])
         own_to_place(m).wait()
 
     def line_sends_end():
@@ -248,11 +259,11 @@
                         cond = exists[dz] if k == 0 else exists[dz] & exists[-k * dz]
                         pl.when(cond)(lambda: await_bytes(own.at[0], send_sem.at[1]))
 
-    own_line(0)
+    own_ring(0)
     for m in range(members):
+        own_line(m)
+    for m in range(1, members):
         own_ring(m)
-    for m in range(1, members):
-        own_line(m)
     for m in range(members):
         own_to_place(m).start()
 
@@ -549,15 +560,12 @@
     work.insert(1, out_work)
     def gather_plan():
         last = members - 1
-        plan = [lambda: column(0, 1), lambda: relay(last, 0)]
-        plan += [lambda: column(last, 1), lambda: relay(0, 0)]
+        plan = [lambda: column(0, 1), lambda: relay(last, 0), lambda: relay(0, 0)]
         for k in range(2, line):
-            plan += [lambda k=k: column(0, k), lambda k=k: across(last, k - 2)]
-            plan += [lambda k=k: column(last, k), lambda k=k: relay(0, k - 1)]
-        plan.append(lambda: relay(0, line - 1))
-        rest = [lambda: across(last, line - 1)]
-        rest += [lambda k=k: relay(last, k) for k in range(1, line)]
-        return plan, rest
+            plan += [lambda k=k: column(0, k), lambda k=k: column(last, k - 1)]
+            plan += [lambda k=k: relay(0, k - 1), lambda k=k: across(last, k - 2)]
+        plan += [lambda: relay(0, line - 1), lambda: column(last, line - 1)]
+        return plan, [lambda: across(last, line - 1)]
 
     before, after = gather_plan()
     while len(work) > len(before):
@@ -674,7 +682,7 @@
             pltpu.VMEM((members, SUB, width), f32),
             pltpu.SemaphoreType.DMA((5,)),
             pltpu.SemaphoreType.DMA((1 + members,)),
-            pltpu.SemaphoreType.DMA((members, 4, line)),
+            pltpu.SemaphoreType.DMA((members, 4, line, levels)),
             pltpu.SemaphoreType.DMA((members,)),
             pltpu.SemaphoreType.DMA((2,)),
             pltpu.SemaphoreType.DMA((1,)),

time: 35.3 us -> 34.8 us (0.986)
  Pallas kernels: 33.2 us -> 32.7 us
    pallas_call x1, Pallas kernels: 33.2 us -> 32.7 us  [on_device(): pl.pallas_call(functools.partial(kernel, num_shot_devices, num_probe_devi...]
where the time goes in v4:
time: 34.8 us; the launch traced here: 34.6 us
  Pallas kernels  32.7 us (94%)
  local copies, waits for them, and re-layouts  1.87 us (5%)
    pallas_call x1, Pallas kernels, on_device(): pl.pallas_call(functools.partial(kernel, num_shot_devices, num_probe_devi...  32.7 us
    unnamed x1, local copies, waits for them, and re-layouts  1.87 us

profile of v4, /device:TPU:1, one launch (start us, length us, event | category | flops | bytes accessed | tf_op | source)
XLA Modules:
  0.0 34.6 jit_solution(13929263192382728201)
XLA Ops:
  0.0 32.7 %shard_map.82 = f32[2,128,512]{2,1,0:T(8,128)} custom-call(s32[33]{0:T(128)} %bounds_ref.1, s32[2,256]{1,0:T(2,128)} %encodings_ref.1, f32[3,256]{1,0:T(4,128)} %wavelet_ref.1, f32[2,256,512]{2,1,0:T(8,128)} %probes_hbm.1, f32[2,128,512]{2,1,0:T(8,128)} %coarse_hbm.1, f32[256,512]{1,0:T(8,128)} %coefficient_hbm.1, f32[256,512]{1,0:T(8,128)} %receiver_hbm.1, ...), custom_call_target="tpu_custom_call" | custom-call | tf_op jit(solution)/shard_map/pallas_call | solution.py:646
  32.7 1.9 %copy.10 = f32[2,128,512]{2,1,0:T(8,128)} copy(f32[2,128,512]{2,1,0:T(8,128)} %shard_map.82) | data formatting | bytes 1048576
